TPU v7x, 256 devices: a whole 4x4x8 slice. The times are simulated.
256 devices in a mesh: seq: 32 (over z, y), chan: 8 (over x, core).
Axes of the slice: x: 4, y: 4, z: 8, core: 2. Of those that a mesh axis runs over, the one named last changes fastest.
Arguments:
- hyena_query: bfloat16 [4096, 8192], P('chan', 'seq'), may hold values from -36 to 36
- hyena_key: bfloat16 [4096, 8192], P('chan', 'seq'), may hold values from -6 to 6
- hyena_value: bfloat16 [4096, 8192], P('chan', 'seq'), may hold values from -6 to 6
- long_filter: float32 [4096, 8192], P(('chan', 'seq')), may hold values from -4 to 4
- skip_weight: float32 [4096], P(('chan', 'seq')), may hold values from 0.5 to 1.5
- stripe_order: int32 [8192], replicated, may hold values from 0 to 8191, as said below
- query_rows: bfloat16 [8192, 4096], P('seq', 'chan'), may hold values from -6 to 6
- key_rows: bfloat16 [8192, 4096], P('seq', 'chan'), may hold values from -6 to 6
- norm_gain: float32 [4096], P('chan'), may hold values from 0.1 to 1.9
Outputs:
- hyena_output: bfloat16 [4096, 8192], P('chan', 'seq')
- attended: bfloat16 [8192, 4096], P('seq', 'chan')
Inputs may be any that keep to these rules, and one draw needn't show every extreme that they name: stripe_order[256 * s + j] = 32 * j + sigma(s) for 0 <= j < 256 and 0 <= s < 32, where sigma is a permutation of 0 to 31.
All inputs are finite; a program needn't handle non-finite values.
Results may differ from a plain program's by a relative error of at most 0.012.
Values may be sent and summed in bfloat16 or wider, within the bound.
No kernel may reach another device: no remote copies, remote signals or barrier semaphores. Data moves between devices by JAX's collectives and lax.ppermute only.
A program may use at most 128 MiB of HBM per device.

v0:
```python
import math
import jax
import jax.numpy as jnp
from jax import lax
from jax.sharding import PartitionSpec as P

D = 4096
HEAD_DIM = 128


def angle_table(first, second, modulus):
    left = jnp.arange(first, dtype=jnp.int32)[:, None]
    right = jnp.arange(second, dtype=jnp.int32)[None, :]
    theta = 2.0 * math.pi / modulus * (left * right % modulus).astype(jnp.float32)
    return (jnp.cos(theta), jnp.sin(theta))


def transform_tables(length):
    outer = 2 * length // 128
    first_cos, first_sin = angle_table(outer, outer // 2, outer)
    twist_cos, twist_sin = angle_table(outer, 128, 2 * length)
    inner_cos, inner_sin = angle_table(128, 128, 128)
    return (first_cos, first_sin, twist_cos, twist_sin, inner_cos, inner_sin)


def contract(form, left, right):
    return jnp.einsum(form, left, right, precision=lax.Precision.HIGHEST)


def forward(signal, tables):
    first_cos, first_sin, twist_cos, twist_sin, inner_cos, inner_sin = tables
    section_real = contract("kt,cts->cks", first_cos, signal)
    section_imag = -contract("kt,cts->cks", first_sin, signal)
    turned_real = section_real * twist_cos + section_imag * twist_sin
    turned_imag = section_imag * twist_cos - section_real * twist_sin
    out_real = contract("cks,sm->ckm", turned_real, inner_cos) + contract(
        "cks,sm->ckm", turned_imag, inner_sin
    )
    out_imag = contract("cks,sm->ckm", turned_imag, inner_cos) - contract(
        "cks,sm->ckm", turned_real, inner_sin
    )
    return (out_real, out_imag)


def inverse(spectrum_real, spectrum_imag, tables):
    first_cos, first_sin, twist_cos, twist_sin, inner_cos, inner_sin = tables
    back_real = contract("ckm,sm->cks", spectrum_real, inner_cos) - contract(
        "ckm,sm->cks", spectrum_imag, inner_sin
    )
    back_imag = contract("ckm,sm->cks", spectrum_real, inner_sin) + contract(
        "ckm,sm->cks", spectrum_imag, inner_cos
    )
    turned_real = back_real * twist_cos - back_imag * twist_sin
    turned_imag = back_real * twist_sin + back_imag * twist_cos
    signal = contract("kt,cks->cts", first_cos, turned_real) - contract(
        "kt,cks->cts", first_sin, turned_imag
    )
    return signal * (1.0 / (first_cos.shape[0] * 128))


def convolve(signal, filter_parts, tables):
    pencil, length = signal.shape
    widened = signal.astype(jnp.float32).reshape(pencil, length // 128, 128)
    signal_real, signal_imag = forward(widened, tables)
    filter_real, filter_imag = filter_parts
    product_real = signal_real * filter_real - signal_imag * filter_imag
    product_imag = signal_real * filter_imag + signal_imag * filter_real
    return inverse(product_real, product_imag, tables).reshape(pencil, length)


def fold_keys(carry, queries, own_places, key_piece, value_piece, places, scale):
    count = key_piece.shape[0]
    heads = queries.shape[1]
    depth = queries.shape[2]
    block = math.gcd(count, 512)
    place_blocks = places.reshape(count // block, block)
    key_blocks = key_piece.reshape(count // block, block, heads, depth)
    value_blocks = value_piece.reshape(count // block, block, heads, depth)

    def one_block(state, inputs):
        running, totals, sums = state
        key_block, value_block, key_places = inputs
        scores = (
            jnp.einsum("qhd,khd->hqk", queries, key_block, preferred_element_type=jnp.float32)
            * scale
        )
        allowed = key_places[None, None, :] <= own_places[None, :, None]
        scores = jnp.where(allowed, scores, -1e30)
        highest = jnp.maximum(running, jnp.max(scores, axis=2))
        weights = jnp.where(allowed, jnp.exp(scores - highest[:, :, None]), 0.0)
        factor = jnp.exp(running - highest)
        totals = totals * factor + jnp.sum(weights, axis=2)
        update = jnp.einsum(
            "hqk,khd->hqd",
            weights.astype(jnp.bfloat16),
            value_block,
            preferred_element_type=jnp.float32,
        )
        sums = sums * factor[:, :, None] + update
        return ((highest, totals, sums), None)

    carry, unused = lax.scan(one_block, carry, (key_blocks, value_blocks, place_blocks))
    return carry


def local(
    hyena_query,
    hyena_key,
    hyena_value,
    long_filter,
    skip_weight,
    stripe_order,
    query_rows,
    key_rows,
    norm_gain,
):
    stripes = lax.axis_size("seq")
    channels, rows = hyena_query.shape
    pencil, length = long_filter.shape
    sigma = stripe_order.reshape(stripes, rows)[:, 0]
    product = (hyena_key.astype(jnp.float32) * hyena_value.astype(jnp.float32)).astype(jnp.bfloat16)
    tables = transform_tables(length)
    filter_parts = forward(long_filter.reshape(pencil, length // 128, 128), tables)
    spread = lax.all_to_all(product, "seq", split_axis=0, concat_axis=1, tiled=True)
    summed = convolve(spread, filter_parts, tables) + skip_weight[:, None] * spread.astype(
        jnp.float32
    )
    returned = lax.all_to_all(
        summed.astype(jnp.bfloat16), "seq", split_axis=1, concat_axis=0, tiled=True
    ).astype(summed.dtype)
    gated = (hyena_query.astype(jnp.float32) * returned).astype(jnp.bfloat16)
    per_stripe = rows // stripes
    columns = stripes * jnp.arange(per_stripe, dtype=jnp.int32)[None, :] + sigma[:, None]
    arranged = jnp.take(gated, columns.reshape(rows), axis=1).reshape(channels, stripes, per_stripe)
    banded = lax.all_to_all(arranged, "seq", split_axis=1, concat_axis=2, tiled=True).reshape(
        channels, rows
    )
    output_wide = banded.astype(jnp.float32)
    squares = lax.psum(jnp.sum(output_wide * output_wide, axis=0), "chan")
    inverse_rms = lax.rsqrt(squares / D + 1e-05)
    normed = (output_wide * inverse_rms[None, :] * norm_gain[:, None]).astype(jnp.bfloat16)
    value_rows = normed.T
    local_heads = channels // HEAD_DIM
    scale = 1.0 / math.sqrt(HEAD_DIM)
    seq_index = lax.axis_index("seq")
    own_places = lax.dynamic_slice_in_dim(stripe_order, seq_index * rows, rows)
    queries = query_rows.reshape(rows, local_heads, HEAD_DIM)
    initial = (
        jnp.full((local_heads, rows), -1e30, jnp.float32),
        jnp.zeros((local_heads, rows), jnp.float32),
        jnp.zeros((local_heads, rows, HEAD_DIM), jnp.float32),
    )
    key_piece = lax.all_gather(key_rows, "seq", axis=0, tiled=True)
    value_piece = lax.all_gather(value_rows, "seq", axis=0, tiled=True)
    running, totals, sums = fold_keys(
        initial, queries, own_places, key_piece, value_piece, stripe_order, scale
    )
    attended = (
        (sums / totals[:, :, None]).transpose(1, 0, 2).reshape(rows, channels).astype(jnp.bfloat16)
    )
    return (banded, attended)


def solution(mesh):
    placed = (
        P("chan", "seq"),
        P("chan", "seq"),
        P("chan", "seq"),
        P(("chan", "seq"), None),
        P(("chan", "seq")),
        P(),
        P("seq", "chan"),
        P("seq", "chan"),
        P("chan"),
    )
    return jax.shard_map(
        local,
        mesh=mesh,
        in_specs=placed,
        out_specs=(P("chan", "seq"), P("seq", "chan")),
        check_vma=False,
    )
```

profile of v0, /device:TPU:1, one launch (start us, length us, event | category | flops | bytes accessed | tf_op | source)
XLA Modules:
  0.0 309.6 jit_solution(8558879919215344293)
XLA Ops:
  7.9 1.8 multiply_convert_fusion.2
  9.7 12.0 %all-to-all-start = ((bf16[32,16,256]{2,1,0:T(8,128)(2,1)}), bf16[32,16,256]{2,1,0:T(8,128)(2,1)S(1)}, u32[]{:S(2)}, u32[]{:S(2)}) async-start(bf16[32,16,256]{2,1,0:T(8,128)(2,1)} %bitcast), calls=%async_computation | async-start | bytes 524288 | tf_op jit(solution)/shard_map/all_to_all | solution.py:124
  22.8 1.2 convolution_negate_fusion
  24.0 1.2 fusion.70
  25.2 1.2 fusion.16
  26.4 1.2 convolution_subtract_fusion.1
  27.7 1.2 fusion.20
  28.9 1.2 convolution_add_fusion.2
  30.1 2.9 all-to-all-done
  34.7 2.0 fusion.34
  36.8 2.2 fusion.35
  39.0 2.0 convolution_add_fusion.3
  41.0 2.2 multiply_add_fusion
  43.2 1.3 fusion.50
  44.5 1.3 fusion.42
  45.8 1.4 convolution_subtract_fusion
  47.1 1.3 convolution_add_fusion.1
  48.5 1.5 fusion.25
  50.0 1.7 fusion.15
  52.9 6.3 %all-to-all-start.1 = ((bf16[16,32,256]{2,0,1:T(8,128)(2,1)}), bf16[16,32,256]{2,0,1:T(8,128)(2,1)S(1)}, u32[]{:S(2)}, u32[]{:S(2)}) async-start(bf16[16,32,256]{2,0,1:T(8,128)(2,1)} %fusion.29), calls=%async_computation.1 | async-start | bytes 524288 | tf_op jit(solution)/shard_map/all_to_all | solution.py:128
  59.4 10.5 %all-to-all-done.1 = bf16[16,32,256]{2,0,1:T(8,128)(2,1)S(1)} async-done(((bf16[16,32,256]{2,0,1:T(8,128)(2,1)}), bf16[16,32,256]{2,0,1:T(8,128)(2,1)S(1)}, u32[]{:S(2)}, u32[]{:S(2)}) %all-to-all-start.1) | async-done | bytes 262176 | tf_op jit(solution)/shard_map/all_to_all | solution.py:128
  70.2 1.2 gather_fusion
  71.5 17.9 %all_to_all.35 = bf16[512,32,8]{0,2,1:T(8,128)(2,1)S(1)} all-to-all(bf16[512,32,8]{0,2,1:T(8,128)(2,1)S(1)} %bitcast_select_fusion.1), channel_id=1, replica_groups=mesh['seq'=32,'chan'=8] {'seq'}, dimensions={1} | all-to-all | bytes 524288 | tf_op jit(solution)/shard_map/all_to_all | solution.py:135
  89.6 16.4 %psum.7 = f32[256]{0:T(256)S(1)} all-reduce(f32[256]{0:T(256)S(1)} %reduce_sum.21), channel_id=1, replica_groups=mesh['seq'=32,'chan'=8] {'chan'}, use_global_device_ids=true, to_apply=%region_1.2 | all-reduce | flops 256 | bytes 2048 | tf_op jit(solution)/shard_map/psum | solution.py:139
  108.8 6.7 %all-gather.3.cloned.1.call-done = bf16[8192,512]{1,0:T(8,128)(2,1)} async-done(((bf16[256,512]{1,0:T(8,128)(2,1)}), bf16[8192,512]{1,0:T(8,128)(2,1)}) %all-gather.3.cloned.1.call-update) | async-done | bytes 8388624 | tf_op jit(solution)/shard_map/all_gather | solution.py:153
  115.6 12.6 %reshape.201 = bf16[16,512,4,128]{3,2,1,0:T(4,128)(2,1)} reshape(bf16[8192,512]{1,0:T(8,128)(2,1)} %all-gather.3.cloned.1.call-done) | data formatting | bytes 16777216 | tf_op jit(solution)/shard_map/reshape | solution.py:77
  128.1 86.4 %all-gather.5.cloned.1.call-done = bf16[8192,512]{1,0:T(8,128)(2,1)} async-done(((bf16[256,512]{1,0:T(8,128)(2,1)}), bf16[8192,512]{1,0:T(8,128)(2,1)}) %all-gather.5.cloned.1.call-update) | async-done | bytes 8388624 | tf_op jit(solution)/shard_map/all_gather | solution.py:154
  214.5 12.5 %reshape.187 = bf16[16,512,4,128]{3,2,1,0:T(4,128)(2,1)} reshape(bf16[8192,512]{1,0:T(8,128)(2,1)} %all-gather.5.cloned.1.call-done) | data formatting | bytes 16777216 | tf_op jit(solution)/shard_map/reshape | solution.py:78
  227.0 74.9 %while.15 = (s32[]{:T(128)}, f32[4,256]{1,0:T(4,128)S(1)}, f32[4,256]{1,0:T(4,128)S(1)}, f32[4,256,128]{2,1,0:T(8,128)S(1)}, s32[16,512]{1,0:T(8,128)}, /*index=...) while((s32[]{:T(128)}, f32[4,256]{1,0:T(4,128)S(1)}, ...), condition=%wide.region_5.6_spmd.clone, body=%wide.region_2.5_spmd.clone.sunk | while | flops 275780608 | bytes 11345025 | solution.py:102
  227.9 1.6 constant_dynamic-slice_fusion.6
  230.5 1.1 convolution_add_fusion.5
  232.6 1.6 constant_dynamic-slice_fusion.6
  235.2 1.1 convolution_add_fusion.5
  237.2 1.6 constant_dynamic-slice_fusion.6
  239.9 1.1 convolution_add_fusion.5
  241.9 1.6 constant_dynamic-slice_fusion.6
  246.6 1.6 constant_dynamic-slice_fusion.6
  251.3 1.6 constant_dynamic-slice_fusion.6
  256.0 1.6 constant_dynamic-slice_fusion.6
  260.6 1.6 constant_dynamic-slice_fusion.6
  265.3 1.6 constant_dynamic-slice_fusion.6
  270.0 1.6 constant_dynamic-slice_fusion.6
  274.7 1.6 constant_dynamic-slice_fusion.6
  279.4 1.6 constant_dynamic-slice_fusion.6
  284.1 1.6 constant_dynamic-slice_fusion.6
  288.7 1.6 constant_dynamic-slice_fusion.6
  293.4 1.6 constant_dynamic-slice_fusion.6
  298.1 1.6 constant_dynamic-slice_fusion.6
  (177 shorter events, 54.5 us)
Async XLA Ops:
  7.2 15.1 %copy-start = (f32[16,8192]{1,0:T(8,128)S(1)}, f32[16,8192]{1,0:T(8,128)}, u32[]{:S(2)}) copy-start(f32[16,8192]{1,0:T(8,128)} %param.14) | copy-start | bytes 1572868
  7.2 15.2 %copy-start.1 = (bf16[512,256]{1,0:T(8,128)(2,1)S(1)}, bf16[512,256]{1,0:T(8,128)(2,1)}, u32[]{:S(2)}) copy-start(bf16[512,256]{1,0:T(8,128)(2,1)} %param.11) | copy-start | bytes 786436
  7.2 15.3 %copy-start.3 = (s32[8192]{0:T(1024)S(1)}, s32[8192]{0:T(1024)}, u32[]{:S(2)}) copy-start(s32[8192]{0:T(1024)} %param.16) | copy-start | bytes 98308
  7.2 108.4 %all-gather.3.cloned.1.call-start = ((), (), s32[]{:S(2)}) async-start(), calls=%async_computation.3 | async-start | bytes 8650752 | tf_op jit(solution)/shard_map/all_gather | solution.py:153
  9.7 23.3 %all-to-all-start = ((bf16[32,16,256]{2,1,0:T(8,128)(2,1)}), bf16[32,16,256]{2,1,0:T(8,128)(2,1)S(1)}, u32[]{:S(2)}, u32[]{:S(2)}) async-start(bf16[32,16,256]{2,1,0:T(8,128)(2,1)} %bitcast), calls=%async_computation | async-start | bytes 524288 | tf_op jit(solution)/shard_map/all_to_all | solution.py:124
  50.0 1.9 copy-start.5
  52.9 17.0 %all-to-all-start.1 = ((bf16[16,32,256]{2,0,1:T(8,128)(2,1)}), bf16[16,32,256]{2,0,1:T(8,128)(2,1)S(1)}, u32[]{:S(2)}, u32[]{:S(2)}) async-start(bf16[16,32,256]{2,0,1:T(8,128)(2,1)} %fusion.29), calls=%async_computation.1 | async-start | bytes 524288 | tf_op jit(solution)/shard_map/all_to_all | solution.py:128
  59.2 155.3 %all-gather.5.cloned.1.call-start = ((), (), s32[]{:S(2)}) async-start(), calls=%async_computation.4 | async-start | bytes 8650752 | tf_op jit(solution)/shard_map/all_gather | solution.py:154
  70.2 35.9 %copy-start.4 = (f32[512]{0:T(512)S(1)}, f32[512]{0:T(512)}, u32[]{:S(2)}) copy-start(f32[512]{0:T(512)} %param.19) | copy-start | bytes 6148
  70.2 37.4 %copy-start.2 = (bf16[256,512]{1,0:T(8,128)(2,1)S(1)}, bf16[256,512]{1,0:T(8,128)(2,1)}, u32[]{:S(2)}) copy-start(bf16[256,512]{1,0:T(8,128)(2,1)} %param.17) | copy-start | bytes 786436
Sparse Core Ops, SparseCore 0:
  10.6 104.9 all-gather.2
  118.7 95.7 all-gather.4
where the time goes:
time: 312 us; the launch traced here: 310 us
  waiting for transfers between devices  107 us (34%)
  local copies, waits for them, and re-layouts  66.1 us (21%)
  matrix products  51.7 us (17%)
  blocking collectives  34.4 us (11%)
  starting transfers between devices  18.4 us (6%)
  other arithmetic  16.6 us (5%)
  between operations  14.4 us (5%)
    all_gather x1, waiting for transfers between devices, local(): value_piece = lax.all_gather(value_rows, 'seq', axis=0, tiled=True)  86.4 us
    dynamic_slice x32, local copies, waits for them, and re-layouts, fold_keys(): lax.scan(one_block, carry, (key_blocks, value_blocks, place_blocks))  36.7 us
    dot_general x18, matrix products, contract(): return jnp.einsum(form, left, right, precision=lax.Precision.HIGHEST)  25.7 us
    all_to_all x1, blocking collectives, local(): lax.all_to_all(arranged, 'seq', split_axis=1, concat_axis=2, tiled=True)  17.9 us
    dot_general x16, matrix products, one_block(): jnp.einsum('hqk,khd->hqd', weights.astype(jnp.bfloat16), value_block, pre...  17.9 us
    psum x1, blocking collectives, local(): squares = lax.psum(jnp.sum(output_wide * output_wide, axis=0), 'chan')  16.4 us
    reshape x1, local copies, waits for them, and re-layouts, fold_keys(): key_blocks = key_piece.reshape(count // block, block, heads, depth)  12.6 us
    reshape x1, local copies, waits for them, and re-layouts, fold_keys(): value_blocks = value_piece.reshape(count // block, block, heads, depth)  12.5 us
  transfers between devices with their start and end apart: 4, of which 4 were waited for; matrix products, arithmetic and copies ran while one was open for 15% of the time, Pallas kernels for 0%

commit v1 on v0

--- a/solution.py
+++ b/solution.py
@@ -3,6 +3,7 @@
 import jax.numpy as jnp
 from jax import lax
 from jax.sharding import PartitionSpec as P
+from jax.lax import all_gather
 
 D = 4096
 HEAD_DIM = 128
@@ -150,8 +151,13 @@
         jnp.zeros((local_heads, rows), jnp.float32),
         jnp.zeros((local_heads, rows, HEAD_DIM), jnp.float32),
     )
-    key_piece = lax.all_gather(key_rows, "seq", axis=0, tiled=True)
-    value_piece = lax.all_gather(value_rows, "seq", axis=0, tiled=True)
+    key_piece, value_piece = jnp.split(
+        all_gather(
+            jnp.concatenate([key_rows, value_rows], axis=1), axis_name="seq", axis=0, tiled=True
+        ),
+        [key_rows.shape[1]],
+        axis=1,
+    )
     running, totals, sums = fold_keys(
         initial, queries, own_places, key_piece, value_piece, stripe_order, scale
     )

time: 312 us -> 362 us (1.16)
  waiting for transfers between devices: 107 us -> 141 us
  local copies, waits for them, and re-layouts: 66.1 us -> 81.1 us
    all_gather x2 -> x1, waiting for transfers between devices: 93.1 us -> 130 us  [local(): all_gather(jnp.concatenate([key_rows, value_rows], axis=1), axis_name='se...]
    split x0 -> x1, local copies, waits for them, and re-layouts: none -> 11.3 us  [local(): jnp.split(all_gather(jnp.concatenate([key_rows, value_rows], axis=1), axi...]
  transfers between devices with their start and end apart: 4 -> 3, of which waited for: 4 -> 2; matrix products, arithmetic and copies ran while one was open for 15% -> 4% of each run, Pallas kernels for 0% -> 0%
where the time goes in v1:
time: 362 us; the launch traced here: 359 us
  waiting for transfers between devices  141 us (39%)
  local copies, waits for them, and re-layouts  81.1 us (22%)
  matrix products  52.5 us (15%)
  blocking collectives  30.8 us (9%)
  starting transfers between devices  21.3 us (6%)
  other arithmetic  17.7 us (5%)
  between operations  14.4 us (4%)
    all_gather x1, waiting for transfers between devices, local(): all_gather(jnp.concatenate([key_rows, value_rows], axis=1), axis_name='se...  130 us
    dynamic_slice x32, local copies, waits for them, and re-layouts, fold_keys(): lax.scan(one_block, carry, (key_blocks, value_blocks, place_blocks))  36.7 us
    dot_general x18, matrix products, contract(): return jnp.einsum(form, left, right, precision=lax.Precision.HIGHEST)  26.5 us
    dot_general x16, matrix products, one_block(): jnp.einsum('hqk,khd->hqd', weights.astype(jnp.bfloat16), value_block, pre...  17.9 us
    psum x1, blocking collectives, local(): squares = lax.psum(jnp.sum(output_wide * output_wide, axis=0), 'chan')  15.5 us
    all_to_all x1, blocking collectives, local(): lax.all_to_all(arranged, 'seq', split_axis=1, concat_axis=2, tiled=True)  15.3 us
    reshape x1, local copies, waits for them, and re-layouts, fold_keys(): key_blocks = key_piece.reshape(count // block, block, heads, depth)  12.6 us
    reshape x1, local copies, waits for them, and re-layouts, fold_keys(): value_blocks = value_piece.reshape(count // block, block, heads, depth)  12.6 us
  transfers between devices with their start and end apart: 3, of which 2 were waited for; matrix products, arithmetic and copies ran while one was open for 4% of the time, Pallas kernels for 0%

profile of v1, /device:TPU:1, one launch (start us, length us, event | category | flops | bytes accessed | tf_op | source)
XLA Modules:
  0.0 359.5 jit_solution(1111706419539439511)
XLA Ops:
  7.2 1.8 multiply_convert_fusion.2
  9.0 12.2 %all-to-all-start = ((bf16[32,16,256]{2,1,0:T(8,128)(2,1)}), bf16[32,16,256]{2,1,0:T(8,128)(2,1)}, u32[]{:S(2)}, u32[]{:S(2)}) async-start(bf16[32,16,256]{2,1,0:T(8,128)(2,1)} %bitcast), calls=%async_computation | async-start | bytes 524288 | tf_op jit(solution)/shard_map/all_to_all | solution.py:125
  21.4 1.1 copy.92
  22.6 1.2 convolution_negate_fusion
  23.7 1.2 fusion.70
  25.1 1.2 fusion.16
  26.3 1.2 convolution_subtract_fusion.1
  27.6 1.8 copy.56
  29.7 1.2 fusion.20
  30.9 2.2 convolution_add_fusion.2
  35.8 2.0 fusion.34
  37.8 2.2 fusion.35
  40.0 2.0 convolution_add_fusion.3
  42.1 2.2 multiply_add_fusion
  44.2 1.3 fusion.50
  45.5 1.3 fusion.42
  46.8 1.3 convolution_subtract_fusion
  48.1 1.3 convolution_add_fusion.1
  49.4 1.5 fusion.25
  50.9 1.7 fusion.15
  52.8 2.0 fusion.29
  54.8 9.1 %all-to-all-start.1 = ((bf16[16,32,256]{2,0,1:T(8,128)(2,1)}), bf16[16,32,256]{2,0,1:T(8,128)(2,1)S(1)}, u32[]{:S(2)}, u32[]{:S(2)}) async-start(bf16[16,32,256]{2,0,1:T(8,128)(2,1)} %fusion.29), calls=%async_computation.1 | async-start | bytes 524288 | tf_op jit(solution)/shard_map/all_to_all | solution.py:129
  64.1 10.5 %all-to-all-done.1 = bf16[16,32,256]{2,0,1:T(8,128)(2,1)S(1)} async-done(((bf16[16,32,256]{2,0,1:T(8,128)(2,1)}), bf16[16,32,256]{2,0,1:T(8,128)(2,1)S(1)}, u32[]{:S(2)}, u32[]{:S(2)}) %all-to-all-start.1) | async-done | bytes 262176 | tf_op jit(solution)/shard_map/all_to_all | solution.py:129
  74.9 1.2 gather_fusion
  76.2 15.3 %all_to_all.35 = bf16[512,32,8]{0,2,1:T(8,128)(2,1)S(1)} all-to-all(bf16[512,32,8]{0,2,1:T(8,128)(2,1)S(1)} %bitcast_select_fusion.1), channel_id=1, replica_groups=mesh['seq'=32,'chan'=8] {'seq'}, dimensions={1} | all-to-all | bytes 524288 | tf_op jit(solution)/shard_map/all_to_all | solution.py:136
  91.7 15.5 %psum.7 = f32[256]{0:T(256)S(1)} all-reduce(f32[256]{0:T(256)S(1)} %reduce_sum.21), channel_id=1, replica_groups=mesh['seq'=32,'chan'=8] {'chan'}, use_global_device_ids=true, to_apply=%region_1.2 | all-reduce | flops 256 | bytes 2048 | tf_op jit(solution)/shard_map/psum | solution.py:140
  110.2 130.2 %all-gather.2.cloned.1.call-done = bf16[8192,1024]{1,0:T(8,128)(2,1)} async-done(((bf16[256,1024]{1,0:T(8,128)(2,1)}), bf16[8192,1024]{1,0:T(8,128)(2,1)}) %all-gather.2.cloned.1.call-update) | async-done | bytes 16777232 | tf_op jit(solution)/shard_map/all_gather | solution.py:155
  240.4 11.3 %fusion.172 = (bf16[8192,512]{1,0:T(8,128)(2,1)}, bf16[8192,512]{1,0:T(8,128)(2,1)}) fusion(bf16[8192,1024]{1,0:T(8,128)(2,1)} %all-gather.2.cloned.1.call-done), kind=kLoop, calls=%fused_computation.209 | loop fusion | bytes 33554432 | tf_op jit(solution)/shard_map/split | solution.py:154
  251.7 12.6 %reshape.185 = bf16[16,512,4,128]{3,2,1,0:T(4,128)(2,1)} reshape(bf16[8192,512]{1,0:T(8,128)(2,1)} %get-tuple-element.138) | data formatting | bytes 16777216 | tf_op jit(solution)/shard_map/reshape | solution.py:78
  264.3 12.6 %reshape.187 = bf16[16,512,4,128]{3,2,1,0:T(4,128)(2,1)} reshape(bf16[8192,512]{1,0:T(8,128)(2,1)} %get-tuple-element.137) | data formatting | bytes 16777216 | tf_op jit(solution)/shard_map/reshape | solution.py:79
  276.8 74.9 %while.15 = (s32[]{:T(128)}, f32[4,256]{1,0:T(4,128)S(1)}, f32[4,256]{1,0:T(4,128)S(1)}, f32[4,256,128]{2,1,0:T(8,128)S(1)}, s32[16,512]{1,0:T(8,128)}, /*index=...) while((s32[]{:T(128)}, f32[4,256]{1,0:T(4,128)S(1)}, ...), condition=%wide.region_5.6_spmd.clone, body=%wide.region_2.5_spmd.clone.sunk | while | flops 275780608 | bytes 11345025 | solution.py:103
  277.7 1.6 constant_dynamic-slice_fusion.6
  280.3 1.1 convolution_add_fusion.5
  282.4 1.6 constant_dynamic-slice_fusion.6
  287.0 1.6 constant_dynamic-slice_fusion.6
  291.7 1.6 constant_dynamic-slice_fusion.6
  296.4 1.6 constant_dynamic-slice_fusion.6
  301.1 1.6 constant_dynamic-slice_fusion.6
  305.8 1.6 constant_dynamic-slice_fusion.6
  310.5 1.6 constant_dynamic-slice_fusion.6
  315.1 1.6 constant_dynamic-slice_fusion.6
  319.8 1.6 constant_dynamic-slice_fusion.6
  324.5 1.6 constant_dynamic-slice_fusion.6
  329.2 1.6 constant_dynamic-slice_fusion.6
  333.9 1.6 constant_dynamic-slice_fusion.6
  338.6 1.6 constant_dynamic-slice_fusion.6
  343.2 1.6 constant_dynamic-slice_fusion.6
  347.9 1.6 constant_dynamic-slice_fusion.6
  (178 shorter events, 55.9 us)
Async XLA Ops:
  9.0 24.2 %all-to-all-start = ((bf16[32,16,256]{2,1,0:T(8,128)(2,1)}), bf16[32,16,256]{2,1,0:T(8,128)(2,1)}, u32[]{:S(2)}, u32[]{:S(2)}) async-start(bf16[32,16,256]{2,1,0:T(8,128)(2,1)} %bitcast), calls=%async_computation | async-start | bytes 524288 | tf_op jit(solution)/shard_map/all_to_all | solution.py:125
  26.3 3.1 copy-start.4
  40.0 2.1 copy-start
  50.9 1.9 copy-start.6
  52.6 22.2 %copy-start.1 = (bf16[512,256]{0,1:T(8,128)(2,1)S(1)}, bf16[512,256]{0,1:T(8,128)(2,1)}, u32[]{:S(2)}) copy-start(bf16[512,256]{0,1:T(8,128)(2,1)} %copy.56) | copy-start | bytes 786436
  54.8 19.8 %all-to-all-start.1 = ((bf16[16,32,256]{2,0,1:T(8,128)(2,1)}), bf16[16,32,256]{2,0,1:T(8,128)(2,1)S(1)}, u32[]{:S(2)}, u32[]{:S(2)}) async-start(bf16[16,32,256]{2,0,1:T(8,128)(2,1)} %fusion.29), calls=%async_computation.1 | async-start | bytes 524288 | tf_op jit(solution)/shard_map/all_to_all | solution.py:129
  63.9 176.5 %all-gather.2.cloned.1.call-start = ((), (), s32[]{:S(2)}) async-start(), calls=%async_computation.3 | async-start | bytes 17301504 | tf_op jit(solution)/shard_map/all_gather | solution.py:155
  74.9 32.4 %copy-start.5 = (f32[512]{0:T(512)S(1)}, f32[512]{0:T(512)}, u32[]{:S(2)}) copy-start(f32[512]{0:T(512)} %param.19) | copy-start | bytes 6148
  74.9 32.5 %copy-start.3 = (bf16[256,512]{1,0:T(8,128)(2,1)S(1)}, bf16[256,512]{1,0:T(8,128)(2,1)}, u32[]{:S(2)}) copy-start(bf16[256,512]{1,0:T(8,128)(2,1)} %param.18) | copy-start | bytes 786436
  76.1 33.0 %copy-start.2 = (bf16[256,512]{1,0:T(8,128)(2,1)S(1)}, bf16[256,512]{1,0:T(8,128)(2,1)}, u32[]{:S(2)}) copy-start(bf16[256,512]{1,0:T(8,128)(2,1)} %param.17) | copy-start | bytes 786436
Sparse Core Ops, SparseCore 0:
  108.5 131.8 all-gather.1
